TPU v7x, 256 devices: a whole 4x4x8 slice. The times are simulated.
256 devices in a mesh: blk: 16 (over y, x_lo, core), inner: 16 (over x_hi, z).
Axes of the slice: x: 4 (x_hi: 2, x_lo: 2; x = x_hi * 2 + x_lo), y: 4, z: 8, core: 2. Of those that a mesh axis runs over, the one named last changes fastest.
Arguments:
- records: float32 [2048, 64, 2048], P('blk', 'inner'), may hold values from -6 to 6
- starts: int32 [64], P('inner'), may hold values from 0 to 1024, as said below
- offsets: int32 [2048, 16], P('blk'), may hold values from -256 to 256, as said below
Outputs:
- correlations: float32 [16, 2048, 768], P('inner', 'blk')
Inputs may be any that keep to these rules, and one draw needn't show every extreme that they name: Segment s uses samples starts[s] to starts[s] + 1023 of its slot. `offsets`: never zero; the partner of channel c is (c + offset) mod 2048.
All inputs are finite; a program needn't handle non-finite values.
Results may differ from a plain program's by a relative error of at most 0.0003.
Values sent between devices are 32-bit elements; how exact they have to be, the bound alone decides.
A program may use at most 128 MiB of HBM per device.

v0:
```python
import math
import jax
import jax.numpy as jnp
from jax import lax
from jax.sharding import PartitionSpec as P

SEG = 1024
LAGS = 768
HALF = 32
PAIRS = 16
F = 512


def shifted(value, axis, steps):
    count = lax.axis_size(axis)
    pairs = [(source, (source + steps) % count) for source in range(count)]
    return lax.ppermute(value, axis, pairs)


def cut_segment(slot_rows, begin):
    return lax.dynamic_slice_in_dim(slot_rows, begin, SEG, 1)


def lag_rows(bin_ids, half_ids, factor):
    shifts = jnp.arange(LAGS, dtype=jnp.int32) - LAGS // 2
    phase = bin_ids[:, None] * shifts[None, :] % SEG
    angle = 2.0 * jnp.pi / SEG * phase.astype(jnp.float32)
    table = jnp.where(half_ids[:, None] == 0, jnp.cos(angle), -jnp.sin(angle))
    return table * factor


def local(records, starts, offsets):
    channels_here = records.shape[0]
    groups = lax.axis_size("inner")
    group_index = lax.axis_index("inner")
    width = F // groups
    samples = jnp.arange(SEG, dtype=jnp.int32)
    window = 0.5 - 0.5 * jnp.cos(2.0 * jnp.pi * samples.astype(jnp.float32) / SEG)
    pieces = jax.vmap(cut_segment, in_axes=(1, 0), out_axes=1)(records, starts) * window
    segment_rows = pieces.reshape(-1, SEG)
    columns = jnp.arange(2 * F, dtype=jnp.int32)
    column_half = columns // width % 2
    column_bin = columns // (2 * width) * width + columns % width
    phase = samples[:, None] * column_bin[None, :] % SEG
    angle = 2.0 * jnp.pi / SEG * phase.astype(jnp.float32)
    forward = jnp.where(column_half[None, :] == 0, jnp.cos(angle), -jnp.sin(angle))
    spectra = jnp.dot(
        segment_rows, forward, precision=lax.Precision.HIGHEST, preferred_element_type=jnp.float32
    )
    split_spectra = spectra.reshape(-1, groups, 2, width)
    real_part = split_spectra[:, :, 0, :].reshape(-1, F)
    imag_part = split_spectra[:, :, 1, :].reshape(-1, F)
    bins = jnp.arange(F, dtype=jnp.int32)
    distance = jnp.abs(bins[:, None] - bins[None, :])
    distance = jnp.minimum(distance, F - distance)
    band = (distance <= HALF).astype(jnp.float32) / (2 * HALF + 1)
    power = real_part * real_part + imag_part * imag_part
    smooth = jnp.dot(
        power, band, precision=lax.Precision.HIGHEST, preferred_element_type=jnp.float32
    )
    scale = lax.rsqrt(smooth + 1e-06)
    whitened = (split_spectra * scale.reshape(-1, groups, 1, width)).reshape(
        channels_here, -1, 2 * F
    )
    owned = lax.all_to_all(whitened, "inner", split_axis=2, concat_axis=1, tiled=True)
    segment_count = owned.shape[1]
    flat_owned = owned.reshape(channels_here, -1)
    lower_blocks = []
    current = flat_owned
    for hop_number in range(2):
        current = shifted(current, "blk", 1)
        lower_blocks.append(current)
    upper_blocks = []
    current = flat_owned
    for hop_number in range(2):
        current = shifted(current, "blk", -1)
        upper_blocks.append(current)
    extended = jnp.concatenate(
        [lower_blocks[1], lower_blocks[0], flat_owned, upper_blocks[0], upper_blocks[1]], 0
    )
    extended = extended.reshape(5 * channels_here, segment_count, 2, width)
    own_spectra = owned.reshape(channels_here, segment_count, 2, width)
    own_re = own_spectra[:, :, 0, :]
    own_im = own_spectra[:, :, 1, :]
    local_ids = jnp.arange(channels_here, dtype=jnp.int32) + 2 * channels_here
    factor = math.sqrt(segment_count / F)
    local_rows = jnp.arange(2 * width, dtype=jnp.int32)
    local_table = lag_rows(group_index * width + local_rows % width, local_rows // width, factor)

    def one_pair(column_offsets):
        partner = extended[local_ids + column_offsets]
        partner_re = partner[:, :, 0, :]
        partner_im = partner[:, :, 1, :]
        cross_re = jnp.sum(own_re * partner_re + own_im * partner_im, axis=1) / segment_count
        cross_im = jnp.sum(own_im * partner_re - own_re * partner_im, axis=1) / segment_count
        return jnp.concatenate([cross_re, cross_im], 1)

    cross = lax.map(one_pair, offsets.T)
    joined = cross.reshape(lax.axis_size("inner") * (PAIRS // groups) * channels_here, 2 * width)
    result = jnp.dot(
        joined, local_table, precision=lax.Precision.HIGHEST, preferred_element_type=jnp.float32
    )
    return lax.psum_scatter(
        result.reshape(lax.axis_size("inner") * (PAIRS // groups), channels_here, LAGS),
        "inner",
        scatter_dimension=0,
        tiled=True,
    )


def solution(mesh):
    placed = (P("blk", "inner", None), P("inner"), P("blk", None))
    return jax.shard_map(
        local, mesh=mesh, in_specs=placed, out_specs=P("inner", "blk", None), check_vma=False
    )
```

profile of v0, /device:TPU:8, one launch (start us, length us, event | category | flops | bytes accessed | tf_op | source)
XLA Modules:
  0.0 740.5 jit_solution(15963438975208695441)
XLA Ops:
  6.7 6.6 copy.60
  13.4 12.7 %while.12 = (s32[]{:T(128)}, f32[4,128,2048]{2,1,0:T(8,128)}, s32[4,3]{1,0:T(4,128)S(1)}, f32[4,128,1024]{2,1,0:T(8,128)S(1)}, s32[]{:T(128)}) while((s32[]{:T(128)}, f32[4,128,2048]{2,1,0:T(8,128)}, s32[4,3]{1,0:T(4,128)S(1)}, f32[4,128,1024]{2,1,0:T(8,128)S(1)}, s32[]{:T(128)}) %tuple.60), condition=%wide.while_cond, body=%wide.while_body.sunk | while | flops 2 | bytes 1048693 | solution.py:21
  29.5 26.0 %fusion.7 = f32[512,16,2,32]{0,3,2,1:T(8,128)S(1)} fusion(f32[512,1024,1,1]{1,0,2,3:T(8,128)} %reshape.238, s32[16,2,32]{2,1,0:T(2,128)S(1)} %fusion.58, pred[16,2,32]{2,1,0:T(4,128)(4,1)S(1)} %fusion.60), kind=kOutput, calls=%fused_computation.22 | convolution fusion | flops 6459228160 | bytes 4199424 | tf_op jit(solution)/shard_map/dot_general | solution.py:47
  58.2 8.8 %copy.47 = f32[512,16,2,32]{3,2,1,0:T(2,128)} copy(f32[512,16,2,32]{0,3,2,1:T(8,128)S(1)} %broadcast_multiply_fusion.2) | data formatting | bytes 4194304 | tf_op jit(solution)/shard_map/mul | solution.py:62
  67.0 9.5 %reshape.201 = f32[128,4,1024]{2,1,0:T(4,128)S(1)} reshape(f32[512,16,2,32]{3,2,1,0:T(2,128)} %copy.47) | data formatting | bytes 4194304 | tf_op jit(solution)/shard_map/reshape | solution.py:62
  79.1 62.0 %all_to_all.15 = f32[128,4,1024]{0,1,2:T(4,128)S(1)} all-to-all(f32[128,4,1024]{0,1,2:T(4,128)} %copy.48), channel_id=1, replica_groups=mesh['blk'=16,'inner'=16] {'inner'}, dimensions={2} | all-to-all | bytes 4194304 | tf_op jit(solution)/shard_map/all_to_all | solution.py:65
  144.2 46.2 %collective-permute-done = f32[128,4096]{0,1:T(8,128)} collective-permute-done((f32[128,4096]{0,1:T(8,128)S(1)}, f32[128,4096]{0,1:T(8,128)}, u32[]{:S(2)}, u32[]{:S(2)}) %collective-permute-start) | collective-permute-done | bytes 2097184 | tf_op jit(solution)/shard_map/ppermute | solution.py:17
  200.3 38.6 %collective-permute-done.1 = f32[128,4096]{0,1:T(8,128)} collective-permute-done((f32[128,4096]{0,1:T(8,128)}, f32[128,4096]{0,1:T(8,128)}, u32[]{:S(2)}, u32[]{:S(2)}) %collective-permute-start.1) | collective-permute-done | bytes 2097184 | tf_op jit(solution)/shard_map/ppermute | solution.py:17
  238.9 3.4 constant_dynamic-update-slice_fusion.4
  242.3 3.4 constant_dynamic-update-slice_fusion.3
  247.4 3.4 constant_dynamic-update-slice_fusion.1
  250.7 3.4 constant_dynamic-update-slice_fusion
  254.1 20.2 %copy.52 = f32[640,64,2,32]{1,3,2,0:T(8,128)} copy(f32[640,64,2,32]{0,3,2,1:T(8,128)} %constant_dynamic-update-slice_fusion) | data formatting | bytes 20971520
  274.3 234.3 %while.13 = (s32[]{:T(128)}, f32[16,128,64]{2,1,0:T(8,128)S(1)}, s32[16,128]{1,0:T(8,128)}, f32[640,64,2,32]{1,3,2,0:T(8,128)}, f32[128,64,32]{1,2,0:T(8,128)S(1)}, /*index=5*/f32[128,64,32]{1,2,0:T(8,128)}, s32[]{:T(128)}) while((s32[]{:T(128)}, f32[16,128,64]{2,1,0:T(8,128)S(1)}, s32[16,128]{1,0:T(8,128)}, ...), condition=%wide.region_3.4_spmd.clone, body=%wide.region_0.3_spmd.clone.sunk | while | flops 2107010 | bytes 8689749 | solution.py:98
  275.0 9.8 %gather_fusion = f32[128,64,2,32]{1,3,2,0:T(8,128)} fusion(f32[640,64,2,32]{1,3,2,0:T(8,128)} %get-tuple-element.249, s32[1024]{0:T(1024)S(1)} %pad_clamp_fusion.2), kind=kCustom, calls=%fused_computation.clone.clone.1 | custom fusion | bytes 4194816 | tf_op jit(solution)/shard_map/while/body/eval_jaxpr/gather | solution.py:91
  284.8 4.1 add_reduce_fusion.2
  289.7 9.8 %gather_fusion = f32[128,64,2,32]{1,3,2,0:T(8,128)} fusion(f32[640,64,2,32]{1,3,2,0:T(8,128)} %get-tuple-element.249, s32[1024]{0:T(1024)S(1)} %pad_clamp_fusion.2), kind=kCustom, calls=%fused_computation.clone.clone.1 | custom fusion | bytes 4194816 | tf_op jit(solution)/shard_map/while/body/eval_jaxpr/gather | solution.py:91
  299.4 4.1 add_reduce_fusion.2
  304.3 9.8 %gather_fusion = f32[128,64,2,32]{1,3,2,0:T(8,128)} fusion(f32[640,64,2,32]{1,3,2,0:T(8,128)} %get-tuple-element.249, s32[1024]{0:T(1024)S(1)} %pad_clamp_fusion.2), kind=kCustom, calls=%fused_computation.clone.clone.1 | custom fusion | bytes 4194816 | tf_op jit(solution)/shard_map/while/body/eval_jaxpr/gather | solution.py:91
  314.1 4.1 add_reduce_fusion.2
  318.9 9.8 %gather_fusion = f32[128,64,2,32]{1,3,2,0:T(8,128)} fusion(f32[640,64,2,32]{1,3,2,0:T(8,128)} %get-tuple-element.249, s32[1024]{0:T(1024)S(1)} %pad_clamp_fusion.2), kind=kCustom, calls=%fused_computation.clone.clone.1 | custom fusion | bytes 4194816 | tf_op jit(solution)/shard_map/while/body/eval_jaxpr/gather | solution.py:91
  328.7 4.1 add_reduce_fusion.2
  333.6 9.8 %gather_fusion = f32[128,64,2,32]{1,3,2,0:T(8,128)} fusion(f32[640,64,2,32]{1,3,2,0:T(8,128)} %get-tuple-element.249, s32[1024]{0:T(1024)S(1)} %pad_clamp_fusion.2), kind=kCustom, calls=%fused_computation.clone.clone.1 | custom fusion | bytes 4194816 | tf_op jit(solution)/shard_map/while/body/eval_jaxpr/gather | solution.py:91
  343.3 4.1 add_reduce_fusion.2
  348.2 9.8 %gather_fusion = f32[128,64,2,32]{1,3,2,0:T(8,128)} fusion(f32[640,64,2,32]{1,3,2,0:T(8,128)} %get-tuple-element.249, s32[1024]{0:T(1024)S(1)} %pad_clamp_fusion.2), kind=kCustom, calls=%fused_computation.clone.clone.1 | custom fusion | bytes 4194816 | tf_op jit(solution)/shard_map/while/body/eval_jaxpr/gather | solution.py:91
  358.0 4.1 add_reduce_fusion.2
  362.9 9.8 %gather_fusion = f32[128,64,2,32]{1,3,2,0:T(8,128)} fusion(f32[640,64,2,32]{1,3,2,0:T(8,128)} %get-tuple-element.249, s32[1024]{0:T(1024)S(1)} %pad_clamp_fusion.2), kind=kCustom, calls=%fused_computation.clone.clone.1 | custom fusion | bytes 4194816 | tf_op jit(solution)/shard_map/while/body/eval_jaxpr/gather | solution.py:91
  372.6 4.1 add_reduce_fusion.2
  377.5 9.8 %gather_fusion = f32[128,64,2,32]{1,3,2,0:T(8,128)} fusion(f32[640,64,2,32]{1,3,2,0:T(8,128)} %get-tuple-element.249, s32[1024]{0:T(1024)S(1)} %pad_clamp_fusion.2), kind=kCustom, calls=%fused_computation.clone.clone.1 | custom fusion | bytes 4194816 | tf_op jit(solution)/shard_map/while/body/eval_jaxpr/gather | solution.py:91
  387.3 4.1 add_reduce_fusion.2
  392.2 9.8 %gather_fusion = f32[128,64,2,32]{1,3,2,0:T(8,128)} fusion(f32[640,64,2,32]{1,3,2,0:T(8,128)} %get-tuple-element.249, s32[1024]{0:T(1024)S(1)} %pad_clamp_fusion.2), kind=kCustom, calls=%fused_computation.clone.clone.1 | custom fusion | bytes 4194816 | tf_op jit(solution)/shard_map/while/body/eval_jaxpr/gather | solution.py:91
  401.9 4.1 add_reduce_fusion.2
  406.8 9.8 %gather_fusion = f32[128,64,2,32]{1,3,2,0:T(8,128)} fusion(f32[640,64,2,32]{1,3,2,0:T(8,128)} %get-tuple-element.249, s32[1024]{0:T(1024)S(1)} %pad_clamp_fusion.2), kind=kCustom, calls=%fused_computation.clone.clone.1 | custom fusion | bytes 4194816 | tf_op jit(solution)/shard_map/while/body/eval_jaxpr/gather | solution.py:91
  416.6 4.1 add_reduce_fusion.2
  421.5 9.8 %gather_fusion = f32[128,64,2,32]{1,3,2,0:T(8,128)} fusion(f32[640,64,2,32]{1,3,2,0:T(8,128)} %get-tuple-element.249, s32[1024]{0:T(1024)S(1)} %pad_clamp_fusion.2), kind=kCustom, calls=%fused_computation.clone.clone.1 | custom fusion | bytes 4194816 | tf_op jit(solution)/shard_map/while/body/eval_jaxpr/gather | solution.py:91
  431.2 4.1 add_reduce_fusion.2
  436.1 9.8 %gather_fusion = f32[128,64,2,32]{1,3,2,0:T(8,128)} fusion(f32[640,64,2,32]{1,3,2,0:T(8,128)} %get-tuple-element.249, s32[1024]{0:T(1024)S(1)} %pad_clamp_fusion.2), kind=kCustom, calls=%fused_computation.clone.clone.1 | custom fusion | bytes 4194816 | tf_op jit(solution)/shard_map/while/body/eval_jaxpr/gather | solution.py:91
  445.9 4.1 add_reduce_fusion.2
  450.7 9.8 %gather_fusion = f32[128,64,2,32]{1,3,2,0:T(8,128)} fusion(f32[640,64,2,32]{1,3,2,0:T(8,128)} %get-tuple-element.249, s32[1024]{0:T(1024)S(1)} %pad_clamp_fusion.2), kind=kCustom, calls=%fused_computation.clone.clone.1 | custom fusion | bytes 4194816 | tf_op jit(solution)/shard_map/while/body/eval_jaxpr/gather | solution.py:91
  460.5 4.1 add_reduce_fusion.2
  465.4 9.8 %gather_fusion = f32[128,64,2,32]{1,3,2,0:T(8,128)} fusion(f32[640,64,2,32]{1,3,2,0:T(8,128)} %get-tuple-element.249, s32[1024]{0:T(1024)S(1)} %pad_clamp_fusion.2), kind=kCustom, calls=%fused_computation.clone.clone.1 | custom fusion | bytes 4194816 | tf_op jit(solution)/shard_map/while/body/eval_jaxpr/gather | solution.py:91
  475.1 4.1 add_reduce_fusion.2
  480.0 9.8 %gather_fusion = f32[128,64,2,32]{1,3,2,0:T(8,128)} fusion(f32[640,64,2,32]{1,3,2,0:T(8,128)} %get-tuple-element.249, s32[1024]{0:T(1024)S(1)} %pad_clamp_fusion.2), kind=kCustom, calls=%fused_computation.clone.clone.1 | custom fusion | bytes 4194816 | tf_op jit(solution)/shard_map/while/body/eval_jaxpr/gather | solution.py:91
  489.8 4.1 add_reduce_fusion.2
  494.7 9.8 %gather_fusion = f32[128,64,2,32]{1,3,2,0:T(8,128)} fusion(f32[640,64,2,32]{1,3,2,0:T(8,128)} %get-tuple-element.249, s32[1024]{0:T(1024)S(1)} %pad_clamp_fusion.2), kind=kCustom, calls=%fused_computation.clone.clone.1 | custom fusion | bytes 4194816 | tf_op jit(solution)/shard_map/while/body/eval_jaxpr/gather | solution.py:91
  504.4 4.1 add_reduce_fusion.2
  508.6 8.7 %fusion.38 = f32[16,128,768]{2,1,0:T(8,128)} fusion(f32[16,128,64]{2,1,0:T(8,128)S(1)} %get-tuple-element.42, s32[768]{0:T(1024)S(1)} %iota_add_fusion, s32[64]{0:T(128)S(1)} %fusion.61, pred[64]{0:T(512)(128)(4,1)S(1)} %fusion.62), kind=kOutput, calls=%fused_computation.63 | convolution fusion | flops 1208795136 | bytes 6819136 | tf_op jit(solution)/shard_map/dot_general | solution.py:100
  517.3 216.1 %reduce-scatter.2.cloned.1.call-done = f32[1,128,768]{2,1,0:T(8,128)} async-done(((f32[16,128,768]{2,1,0:T(8,128)}), f32[1,128,768]{2,1,0:T(8,128)}) %reduce-scatter.2.cloned.1.call-update) | async-done | bytes 393232 | tf_op jit(solution)/shard_map/reduce_scatter | solution.py:103
  (117 shorter events, 49.1 us)
Async XLA Ops:
  6.5 726.9 %reduce-scatter.2.cloned.1.call-start = ((), (), s32[]{:S(2)}) async-start(), calls=%async_computation.2 | async-start | bytes 6684672 | tf_op jit(solution)/shard_map/reduce_scatter | solution.py:103
  6.7 6.6 copy-start.3
  141.4 52.9 %copy-start = (f32[128,16,4,64]{0,3,2,1:T(8,128)}, f32[128,16,4,64]{0,3,2,1:T(8,128)S(1)}, u32[]{:S(2)}) copy-start(f32[128,16,4,64]{0,3,2,1:T(8,128)S(1)} %copy.50) | copy-start | bytes 6291460
  141.5 48.9 %collective-permute-start = (f32[128,4096]{0,1:T(8,128)S(1)}, f32[128,4096]{0,1:T(8,128)}, u32[]{:S(2)}, u32[]{:S(2)}) collective-permute-start(f32[128,4096]{0,1:T(8,128)S(1)} %bitcast.78), channel_id=1, source_target_pairs={{0,16},{16,32},{32,48},{48,64},{64,80},{80,96},{96,112},{112,128},... | collective-permute-start | bytes 6291464 | tf_op jit(solution)/shard_map/ppermute | solution.py:17
  141.5 48.8 %collective-permute-start.2 = (f32[128,4096]{0,1:T(8,128)S(1)}, f32[128,4096]{0,1:T(8,128)}, u32[]{:S(2)}, u32[]{:S(2)}) collective-permute-start(f32[128,4096]{0,1:T(8,128)S(1)} %bitcast.79), channel_id=1, source_target_pairs={{0,240},{16,0},{32,16},{48,32},{64,48},{80,64},{96,80},{112,96},{1... | collective-permute-start | bytes 6291464 | tf_op jit(solution)/shard_map/ppermute | solution.py:17
  190.3 48.6 %collective-permute-start.1 = (f32[128,4096]{0,1:T(8,128)}, f32[128,4096]{0,1:T(8,128)}, u32[]{:S(2)}, u32[]{:S(2)}) collective-permute-start(f32[128,4096]{0,1:T(8,128)} %collective-permute-done), channel_id=1, source_target_pairs={{0,16},{16,32},{32,48},{48,64},{64,80},{80,96},{96,112},{112,128},... | collective-permute-start | bytes 6291464 | tf_op jit(solution)/shard_map/ppermute | solution.py:17
  190.3 60.4 %collective-permute-start.3 = (f32[128,4096]{0,1:T(8,128)}, f32[128,4096]{0,1:T(8,128)}, u32[]{:S(2)}, u32[]{:S(2)}) collective-permute-start(f32[128,4096]{0,1:T(8,128)} %collective-permute-done.2), channel_id=1, source_target_pairs={{0,240},{16,0},{32,16},{48,32},{64,48},{80,64},{96,80},{112,96},{1... | collective-permute-start | bytes 6291464 | tf_op jit(solution)/shard_map/ppermute | solution.py:17
  242.3 3.4 copy-start.1
  254.1 20.2 %copy-start.2 = (f32[16,128,64]{2,1,0:T(8,128)S(1)}, f32[16,128,64]{2,1,0:T(8,128)}, u32[]{:S(2)}) copy-start(f32[16,128,64]{2,1,0:T(8,128)} %custom-call.4) | copy-start | bytes 1572868
Sparse Core Ops, SparseCore 0:
  517.4 215.9 reduce-scatter.1
where the time goes:
time: 747 us; the launch traced here: 741 us
  waiting for transfers between devices  301 us (40%)
  local copies, waits for them, and re-layouts  242 us (32%)
  other arithmetic  78.7 us (11%)
  blocking collectives  62 us (8%)
  matrix products  36.8 us (5%)
  between operations  13.8 us (2%)
    reduce_scatter x1, waiting for transfers between devices, local(): lax.psum_scatter(result.reshape(lax.axis_size('inner') * (PAIRS // groups...  216 us
    gather x16, local copies, waits for them, and re-layouts, one_pair(): partner = extended[local_ids + column_offsets]  156 us
    ppermute x4, waiting for transfers between devices, shifted(): return lax.ppermute(value, axis, pairs)  84.8 us
    reduce_sum x16, other arithmetic, one_pair(): jnp.sum(own_re * partner_re + own_im * partner_im, axis=1) / segment_count  64.9 us
    all_to_all x1, blocking collectives, local(): lax.all_to_all(whitened, 'inner', split_axis=2, concat_axis=1, tiled=True)  62 us
    unnamed x18, local copies, waits for them, and re-layouts  44.6 us
    dot_general x1, matrix products, local(): jnp.dot(segment_rows, forward, precision=lax.Precision.HIGHEST, preferred...  26 us
  transfers between devices with their start and end apart: 5, of which 3 were waited for; matrix products, arithmetic and copies ran while one was open for 3% of the time, Pallas kernels for 0%

commit v1 on v0

--- a/solution.py
+++ b/solution.py
@@ -62,7 +62,12 @@
     whitened = (split_spectra * scale.reshape(-1, groups, 1, width)).reshape(
         channels_here, -1, 2 * F
     )
-    owned = lax.all_to_all(whitened, "inner", split_axis=2, concat_axis=1, tiled=True)
+    owned = jnp.concatenate(
+        lax.all_to_all(
+            jnp.stack(jnp.split(whitened, lax.axis_size("inner"), axis=2)), "inner", 0, 0
+        ),
+        axis=1,
+    )
     segment_count = owned.shape[1]
     flat_owned = owned.reshape(channels_here, -1)
     lower_blocks = []

time: 747 us -> 762 us (1.020)
  local copies, waits for them, and re-layouts: 242 us -> 258 us
    unnamed x18 -> x33, local copies, waits for them, and re-layouts: 44.6 us -> 57.1 us
where the time goes in v1:
time: 762 us; the launch traced here: 755 us
  waiting for transfers between devices  301 us (40%)
  local copies, waits for them, and re-layouts  258 us (34%)
  other arithmetic  78.7 us (10%)
  blocking collectives  62 us (8%)
  matrix products  36.8 us (5%)
  between operations  13.8 us (2%)
    reduce_scatter x1, waiting for transfers between devices, local(): lax.psum_scatter(result.reshape(lax.axis_size('inner') * (PAIRS // groups...  216 us
    gather x16, local copies, waits for them, and re-layouts, one_pair(): partner = extended[local_ids + column_offsets]  156 us
    ppermute x4, waiting for transfers between devices, shifted(): return lax.ppermute(value, axis, pairs)  84.8 us
    reduce_sum x16, other arithmetic, one_pair(): jnp.sum(own_re * partner_re + own_im * partner_im, axis=1) / segment_count  64.9 us
    all_to_all x1, blocking collectives, local(): lax.all_to_all(jnp.stack(jnp.split(whitened, lax.axis_size('inner'), axis...  62 us
    unnamed x33, local copies, waits for them, and re-layouts  57.1 us
    dot_general x1, matrix products, local(): jnp.dot(segment_rows, forward, precision=lax.Precision.HIGHEST, preferred...  26 us
  transfers between devices with their start and end apart: 5, of which 3 were waited for; matrix products, arithmetic and copies ran while one was open for 3% of the time, Pallas kernels for 0%

profile of v1, /device:TPU:8, one launch (start us, length us, event | category | flops | bytes accessed | tf_op | source)
XLA Modules:
  0.0 755.5 jit_solution(12489568024075911792)
XLA Ops:
  6.7 6.6 copy.33
  13.4 12.7 %while.12 = (s32[]{:T(128)}, f32[4,128,2048]{2,1,0:T(8,128)}, s32[4,3]{1,0:T(4,128)S(1)}, f32[4,128,1024]{2,1,0:T(8,128)S(1)}, s32[]{:T(128)}) while((s32[]{:T(128)}, f32[4,128,2048]{2,1,0:T(8,128)}, s32[4,3]{1,0:T(4,128)S(1)}, f32[4,128,1024]{2,1,0:T(8,128)S(1)}, s32[]{:T(128)}) %tuple.56), condition=%wide.while_cond, body=%wide.while_body.sunk | while | flops 2 | bytes 1048693 | solution.py:21
  29.5 26.0 %fusion.7 = f32[512,16,2,32]{0,3,2,1:T(8,128)S(1)} fusion(f32[512,1024,1,1]{1,0,2,3:T(8,128)} %reshape.235, s32[16,2,32]{2,1,0:T(2,128)S(1)} %fusion.74, pred[16,2,32]{2,1,0:T(4,128)(4,1)S(1)} %fusion.76), kind=kOutput, calls=%fused_computation.22 | convolution fusion | flops 6459228160 | bytes 4199424 | tf_op jit(solution)/shard_map/dot_general | solution.py:47
  58.2 8.8 %copy.23 = f32[512,16,2,32]{3,2,1,0:T(2,128)} copy(f32[512,16,2,32]{0,3,2,1:T(8,128)S(1)} %broadcast_multiply_fusion.2) | data formatting | bytes 4194304 | tf_op jit(solution)/shard_map/mul | solution.py:62
  67.0 9.5 %reshape.198 = f32[128,4,1024]{2,1,0:T(4,128)S(1)} reshape(f32[512,16,2,32]{3,2,1,0:T(2,128)} %copy.23) | data formatting | bytes 4194304 | tf_op jit(solution)/shard_map/reshape | solution.py:62
  90.0 4.8 copy.24
  94.7 62.0 %all_to_all.5 = f32[16,128,4,64]{1,3,2,0:T(8,128)S(1)} all-to-all(f32[16,128,4,64]{1,3,2,0:T(8,128)} %copy.24), channel_id=1, replica_groups=mesh['blk'=16,'inner'=16] {'inner'}, dimensions={0} | all-to-all | bytes 4194304 | tf_op jit(solution)/shard_map/all_to_all | solution.py:66
  159.3 46.2 %collective-permute-done = f32[128,4096]{0,1:T(8,128)} collective-permute-done((f32[128,4096]{0,1:T(8,128)S(1)}, f32[128,4096]{0,1:T(8,128)}, u32[]{:S(2)}, u32[]{:S(2)}) %collective-permute-start) | collective-permute-done | bytes 2097184 | tf_op jit(solution)/shard_map/ppermute | solution.py:17
  215.5 38.6 %collective-permute-done.1 = f32[128,4096]{0,1:T(8,128)} collective-permute-done((f32[128,4096]{0,1:T(8,128)}, f32[128,4096]{0,1:T(8,128)}, u32[]{:S(2)}, u32[]{:S(2)}) %collective-permute-start.1) | collective-permute-done | bytes 2097184 | tf_op jit(solution)/shard_map/ppermute | solution.py:17
  254.1 3.5 constant_dynamic-update-slice_fusion.4
  262.5 3.4 constant_dynamic-update-slice_fusion.1
  265.9 3.4 constant_dynamic-update-slice_fusion
  269.3 20.2 %copy.25 = f32[640,64,2,32]{1,3,2,0:T(8,128)} copy(f32[640,64,2,32]{0,3,2,1:T(8,128)} %constant_dynamic-update-slice_fusion) | data formatting | bytes 20971520
  289.5 234.3 %while.13 = (s32[]{:T(128)}, f32[16,128,64]{2,1,0:T(8,128)S(1)}, s32[16,128]{1,0:T(8,128)}, f32[640,64,2,32]{1,3,2,0:T(8,128)}, f32[128,64,32]{1,2,0:T(8,128)S(1)}, /*index=5*/f32[128,64,32]{1,2,0:T(8,128)}, s32[]{:T(128)}) while((s32[]{:T(128)}, f32[16,128,64]{2,1,0:T(8,128)S(1)}, s32[16,128]{1,0:T(8,128)}, ...), condition=%wide.region_3.4_spmd.clone, body=%wide.region_0.3_spmd.clone.sunk | while | flops 2107010 | bytes 8689749 | solution.py:103
  290.2 9.8 %gather_fusion = f32[128,64,2,32]{1,3,2,0:T(8,128)} fusion(f32[640,64,2,32]{1,3,2,0:T(8,128)} %get-tuple-element.229, s32[1024]{0:T(1024)S(1)} %pad_clamp_fusion.2), kind=kCustom, calls=%fused_computation.clone.clone.1 | custom fusion | bytes 4194816 | tf_op jit(solution)/shard_map/while/body/eval_jaxpr/gather | solution.py:96
  299.9 4.1 add_reduce_fusion.2
  304.8 9.8 %gather_fusion = f32[128,64,2,32]{1,3,2,0:T(8,128)} fusion(f32[640,64,2,32]{1,3,2,0:T(8,128)} %get-tuple-element.229, s32[1024]{0:T(1024)S(1)} %pad_clamp_fusion.2), kind=kCustom, calls=%fused_computation.clone.clone.1 | custom fusion | bytes 4194816 | tf_op jit(solution)/shard_map/while/body/eval_jaxpr/gather | solution.py:96
  314.6 4.1 add_reduce_fusion.2
  319.5 9.8 %gather_fusion = f32[128,64,2,32]{1,3,2,0:T(8,128)} fusion(f32[640,64,2,32]{1,3,2,0:T(8,128)} %get-tuple-element.229, s32[1024]{0:T(1024)S(1)} %pad_clamp_fusion.2), kind=kCustom, calls=%fused_computation.clone.clone.1 | custom fusion | bytes 4194816 | tf_op jit(solution)/shard_map/while/body/eval_jaxpr/gather | solution.py:96
  329.2 4.1 add_reduce_fusion.2
  334.1 9.8 %gather_fusion = f32[128,64,2,32]{1,3,2,0:T(8,128)} fusion(f32[640,64,2,32]{1,3,2,0:T(8,128)} %get-tuple-element.229, s32[1024]{0:T(1024)S(1)} %pad_clamp_fusion.2), kind=kCustom, calls=%fused_computation.clone.clone.1 | custom fusion | bytes 4194816 | tf_op jit(solution)/shard_map/while/body/eval_jaxpr/gather | solution.py:96
  343.9 4.1 add_reduce_fusion.2
  348.8 9.8 %gather_fusion = f32[128,64,2,32]{1,3,2,0:T(8,128)} fusion(f32[640,64,2,32]{1,3,2,0:T(8,128)} %get-tuple-element.229, s32[1024]{0:T(1024)S(1)} %pad_clamp_fusion.2), kind=kCustom, calls=%fused_computation.clone.clone.1 | custom fusion | bytes 4194816 | tf_op jit(solution)/shard_map/while/body/eval_jaxpr/gather | solution.py:96
  358.5 4.1 add_reduce_fusion.2
  363.4 9.8 %gather_fusion = f32[128,64,2,32]{1,3,2,0:T(8,128)} fusion(f32[640,64,2,32]{1,3,2,0:T(8,128)} %get-tuple-element.229, s32[1024]{0:T(1024)S(1)} %pad_clamp_fusion.2), kind=kCustom, calls=%fused_computation.clone.clone.1 | custom fusion | bytes 4194816 | tf_op jit(solution)/shard_map/while/body/eval_jaxpr/gather | solution.py:96
  373.1 4.1 add_reduce_fusion.2
  378.0 9.8 %gather_fusion = f32[128,64,2,32]{1,3,2,0:T(8,128)} fusion(f32[640,64,2,32]{1,3,2,0:T(8,128)} %get-tuple-element.229, s32[1024]{0:T(1024)S(1)} %pad_clamp_fusion.2), kind=kCustom, calls=%fused_computation.clone.clone.1 | custom fusion | bytes 4194816 | tf_op jit(solution)/shard_map/while/body/eval_jaxpr/gather | solution.py:96
  387.8 4.1 add_reduce_fusion.2
  392.7 9.8 %gather_fusion = f32[128,64,2,32]{1,3,2,0:T(8,128)} fusion(f32[640,64,2,32]{1,3,2,0:T(8,128)} %get-tuple-element.229, s32[1024]{0:T(1024)S(1)} %pad_clamp_fusion.2), kind=kCustom, calls=%fused_computation.clone.clone.1 | custom fusion | bytes 4194816 | tf_op jit(solution)/shard_map/while/body/eval_jaxpr/gather | solution.py:96
  402.4 4.1 add_reduce_fusion.2
  407.3 9.8 %gather_fusion = f32[128,64,2,32]{1,3,2,0:T(8,128)} fusion(f32[640,64,2,32]{1,3,2,0:T(8,128)} %get-tuple-element.229, s32[1024]{0:T(1024)S(1)} %pad_clamp_fusion.2), kind=kCustom, calls=%fused_computation.clone.clone.1 | custom fusion | bytes 4194816 | tf_op jit(solution)/shard_map/while/body/eval_jaxpr/gather | solution.py:96
  417.1 4.1 add_reduce_fusion.2
  422.0 9.8 %gather_fusion = f32[128,64,2,32]{1,3,2,0:T(8,128)} fusion(f32[640,64,2,32]{1,3,2,0:T(8,128)} %get-tuple-element.229, s32[1024]{0:T(1024)S(1)} %pad_clamp_fusion.2), kind=kCustom, calls=%fused_computation.clone.clone.1 | custom fusion | bytes 4194816 | tf_op jit(solution)/shard_map/while/body/eval_jaxpr/gather | solution.py:96
  431.7 4.1 add_reduce_fusion.2
  436.6 9.8 %gather_fusion = f32[128,64,2,32]{1,3,2,0:T(8,128)} fusion(f32[640,64,2,32]{1,3,2,0:T(8,128)} %get-tuple-element.229, s32[1024]{0:T(1024)S(1)} %pad_clamp_fusion.2), kind=kCustom, calls=%fused_computation.clone.clone.1 | custom fusion | bytes 4194816 | tf_op jit(solution)/shard_map/while/body/eval_jaxpr/gather | solution.py:96
  446.4 4.1 add_reduce_fusion.2
  451.3 9.8 %gather_fusion = f32[128,64,2,32]{1,3,2,0:T(8,128)} fusion(f32[640,64,2,32]{1,3,2,0:T(8,128)} %get-tuple-element.229, s32[1024]{0:T(1024)S(1)} %pad_clamp_fusion.2), kind=kCustom, calls=%fused_computation.clone.clone.1 | custom fusion | bytes 4194816 | tf_op jit(solution)/shard_map/while/body/eval_jaxpr/gather | solution.py:96
  461.0 4.1 add_reduce_fusion.2
  465.9 9.8 %gather_fusion = f32[128,64,2,32]{1,3,2,0:T(8,128)} fusion(f32[640,64,2,32]{1,3,2,0:T(8,128)} %get-tuple-element.229, s32[1024]{0:T(1024)S(1)} %pad_clamp_fusion.2), kind=kCustom, calls=%fused_computation.clone.clone.1 | custom fusion | bytes 4194816 | tf_op jit(solution)/shard_map/while/body/eval_jaxpr/gather | solution.py:96
  475.7 4.1 add_reduce_fusion.2
  480.5 9.8 %gather_fusion = f32[128,64,2,32]{1,3,2,0:T(8,128)} fusion(f32[640,64,2,32]{1,3,2,0:T(8,128)} %get-tuple-element.229, s32[1024]{0:T(1024)S(1)} %pad_clamp_fusion.2), kind=kCustom, calls=%fused_computation.clone.clone.1 | custom fusion | bytes 4194816 | tf_op jit(solution)/shard_map/while/body/eval_jaxpr/gather | solution.py:96
  490.3 4.1 add_reduce_fusion.2
  495.2 9.8 %gather_fusion = f32[128,64,2,32]{1,3,2,0:T(8,128)} fusion(f32[640,64,2,32]{1,3,2,0:T(8,128)} %get-tuple-element.229, s32[1024]{0:T(1024)S(1)} %pad_clamp_fusion.2), kind=kCustom, calls=%fused_computation.clone.clone.1 | custom fusion | bytes 4194816 | tf_op jit(solution)/shard_map/while/body/eval_jaxpr/gather | solution.py:96
  504.9 4.1 add_reduce_fusion.2
  509.8 9.8 %gather_fusion = f32[128,64,2,32]{1,3,2,0:T(8,128)} fusion(f32[640,64,2,32]{1,3,2,0:T(8,128)} %get-tuple-element.229, s32[1024]{0:T(1024)S(1)} %pad_clamp_fusion.2), kind=kCustom, calls=%fused_computation.clone.clone.1 | custom fusion | bytes 4194816 | tf_op jit(solution)/shard_map/while/body/eval_jaxpr/gather | solution.py:96
  519.6 4.1 add_reduce_fusion.2
  523.8 8.7 %fusion.54 = f32[16,128,768]{2,1,0:T(8,128)} fusion(f32[16,128,64]{2,1,0:T(8,128)S(1)} %get-tuple-element.42, s32[768]{0:T(1024)S(1)} %iota_add_fusion, s32[64]{0:T(128)S(1)} %fusion.77, pred[64]{0:T(512)(128)(4,1)S(1)} %fusion.78), kind=kOutput, calls=%fused_computation.95 | convolution fusion | flops 1208795136 | bytes 6819136 | tf_op jit(solution)/shard_map/dot_general | solution.py:105
  532.5 215.9 %reduce-scatter.2.cloned.1.call-done = f32[1,128,768]{2,1,0:T(8,128)} async-done(((f32[16,128,768]{2,1,0:T(8,128)}), f32[1,128,768]{2,1,0:T(8,128)}) %reduce-scatter.2.cloned.1.call-update) | async-done | bytes 393232 | tf_op jit(solution)/shard_map/reduce_scatter | solution.py:108
  (131 shorter events, 62.7 us)
Async XLA Ops:
  6.5 741.9 %reduce-scatter.2.cloned.1.call-start = ((), (), s32[]{:S(2)}) async-start(), calls=%async_computation.2 | async-start | bytes 6684672 | tf_op jit(solution)/shard_map/reduce_scatter | solution.py:108
  6.7 6.6 copy-start.3
  156.7 52.9 %copy-start = (f32[16,128,4,64]{1,3,2,0:T(8,128)}, f32[16,128,4,64]{1,3,2,0:T(8,128)S(1)}, u32[]{:S(2)}) copy-start(f32[16,128,4,64]{1,3,2,0:T(8,128)S(1)} %all_to_all.5) | copy-start | bytes 6291460
  156.7 48.8 %collective-permute-start = (f32[128,4096]{0,1:T(8,128)S(1)}, f32[128,4096]{0,1:T(8,128)}, u32[]{:S(2)}, u32[]{:S(2)}) collective-permute-start(f32[128,4096]{0,1:T(8,128)S(1)} %bitcast.142), channel_id=1, source_target_pairs={{0,16},{16,32},{32,48},{48,64},{64,80},{80,96},{96,112},{112,128},... | collective-permute-start | bytes 6291464 | tf_op jit(solution)/shard_map/ppermute | solution.py:17
  156.7 48.8 %collective-permute-start.2 = (f32[128,4096]{0,1:T(8,128)S(1)}, f32[128,4096]{0,1:T(8,128)}, u32[]{:S(2)}, u32[]{:S(2)}) collective-permute-start(f32[128,4096]{0,1:T(8,128)S(1)} %bitcast.143), channel_id=1, source_target_pairs={{0,240},{16,0},{32,16},{48,32},{64,48},{80,64},{96,80},{112,96},{1... | collective-permute-start | bytes 6291464 | tf_op jit(solution)/shard_map/ppermute | solution.py:17
  205.5 48.6 %collective-permute-start.1 = (f32[128,4096]{0,1:T(8,128)}, f32[128,4096]{0,1:T(8,128)}, u32[]{:S(2)}, u32[]{:S(2)}) collective-permute-start(f32[128,4096]{0,1:T(8,128)} %collective-permute-done), channel_id=1, source_target_pairs={{0,16},{16,32},{32,48},{48,64},{64,80},{80,96},{96,112},{112,128},... | collective-permute-start | bytes 6291464 | tf_op jit(solution)/shard_map/ppermute | solution.py:17
  205.5 60.4 %collective-permute-start.3 = (f32[128,4096]{0,1:T(8,128)}, f32[128,4096]{0,1:T(8,128)}, u32[]{:S(2)}, u32[]{:S(2)}) collective-permute-start(f32[128,4096]{0,1:T(8,128)} %collective-permute-done.2), channel_id=1, source_target_pairs={{0,240},{16,0},{32,16},{48,32},{64,48},{80,64},{96,80},{112,96},{1... | collective-permute-start | bytes 6291464 | tf_op jit(solution)/shard_map/ppermute | solution.py:17
  254.1 6.8 copy-start.1
  269.3 20.2 %copy-start.2 = (f32[16,128,64]{2,1,0:T(8,128)S(1)}, f32[16,128,64]{2,1,0:T(8,128)}, u32[]{:S(2)}) copy-start(f32[16,128,64]{2,1,0:T(8,128)} %custom-call.5) | copy-start | bytes 1572868
Sparse Core Ops, SparseCore 0:
  532.6 215.7 reduce-scatter.1
